TPU v7x, 32 devices: a whole 2x2x4 slice. The times are simulated.
32 devices in a mesh: groups: 2 (over y), wide: 4 (over z), narrow: 2 (over x), section: 2 (over core).
Axes of the slice: x: 2, y: 2, z: 4, core: 2. Of those that a mesh axis runs over, the one named last changes fastest.
Arguments:
- tokens: bfloat16 [1024, 4096], P(('groups', 'wide', 'section'), 'narrow'), parts along dimension 0, may hold values from -6 to 6
- route_logits: float32 [1024, 8], P(('groups', 'wide', 'section')), parts along dimension 0, may hold values from -8 to 8
- expert_ids: int32 [1024, 8], P(('groups', 'wide', 'section')), parts along dimension 0, may hold values from 0 to 63, all different within a row; in each aligned block of 64 rows (0 to 63, 64 to 127, ...) at most 12 rows name the same one
- gate_weight: bfloat16 [64, 4096, 768], P(('wide', 'section'), None, 'narrow'), may hold values from -0.09375 to 0.09375
- up_weight: bfloat16 [64, 4096, 768], P(('wide', 'section'), None, 'narrow'), may hold values from -0.09375 to 0.09375
- down_weight: bfloat16 [64, 768, 4096], P(('wide', 'section'), None, 'narrow'), may hold values from -0.21875 to 0.21875
Outputs:
- mixed: bfloat16 [1024, 4096], P(('groups', 'wide', 'section'), 'narrow'), parts along dimension 0
There are 2 independent parts, one for each index of `groups`. A program takes and returns all parts, laid end to end along the dimension named above; an argument that names none is the same for every part. Nothing has to cross between parts.
Inputs may be any that keep to these rules, and one draw needn't show every extreme that they name: `expert_ids`: each row names 8 different experts; among the 64 rows of one aligned block no expert is named more than 12 times, a bound that some block reaches.
All inputs are finite; a program needn't handle non-finite values.
Results may differ from a plain program's by a relative error of at most 0.0085.
Values may be sent and summed in bfloat16 or wider, within the bound.
No kernel may reach another device: no remote copies, remote signals or barrier semaphores. Data moves between devices by JAX's collectives and lax.ppermute only.
A program may use at most 128 MiB of HBM per device.

v0:
```python
import jax
import jax.numpy as jnp
from jax import lax
from jax.sharding import PartitionSpec as P

CAP = 12


def shards(tokens, route_logits, expert_ids, gate_weight, up_weight, down_weight):
    tok_rows = tokens.shape[0]
    top_count = expert_ids.shape[1]
    feature_part = tokens.shape[1]
    wide_count = lax.axis_size("wide")
    section_count = lax.axis_size("section")
    owners = wide_count * section_count
    per_owner = gate_weight.shape[0]
    experts = owners * per_owner
    scores = jax.nn.sigmoid(route_logits)
    shares = (scores / jnp.sum(scores, axis=1, keepdims=True)).astype(jnp.bfloat16)
    flat_ids = expert_ids.reshape(-1)
    one_hot = (flat_ids[:, None] == jnp.arange(experts, dtype=jnp.int32)[None, :]).astype(jnp.int32)
    slot_rank = jnp.sum(jnp.cumsum(one_hot, axis=0) * one_hot, axis=1) - 1
    columns = flat_ids * CAP + slot_rank
    placed = (columns[:, None] == jnp.arange(experts * CAP, dtype=jnp.int32)[None, :]).reshape(
        tok_rows, top_count, experts * CAP
    )
    dispatch = jnp.any(placed, axis=1).astype(jnp.bfloat16)
    outgoing = jnp.einsum("rs,rd->sd", dispatch, tokens, preferred_element_type=jnp.float32).astype(
        jnp.bfloat16
    )
    combine = jnp.sum(
        jnp.where(placed, shares.astype(jnp.float32)[:, :, None], 0.0), axis=1
    ).astype(jnp.bfloat16)
    arrived = lax.all_to_all(
        outgoing.reshape(owners, per_owner, CAP, feature_part),
        ("wide", "section"),
        split_axis=0,
        concat_axis=0,
        tiled=True,
    )
    portion = lax.all_gather(arrived, "narrow", axis=3, tiled=True)
    gate_add = jnp.einsum(
        "gjcd,jdf->gjcf", portion, gate_weight, preferred_element_type=jnp.float32
    )
    up_add = jnp.einsum("gjcd,jdf->gjcf", portion, up_weight, preferred_element_type=jnp.float32)
    hidden = (jax.nn.silu(gate_add) * up_add).astype(jnp.bfloat16)
    summed = jnp.einsum(
        "gjcf,jfd->gjcd",
        lax.all_gather(hidden, "narrow", axis=3, tiled=True),
        down_weight,
        preferred_element_type=jnp.float32,
    ).astype(jnp.bfloat16)
    returned = lax.all_to_all(summed, ("wide", "section"), split_axis=0, concat_axis=0, tiled=True)
    returned = returned.reshape(experts * CAP, feature_part)
    return jnp.dot(combine, returned, preferred_element_type=jnp.float32).astype(jnp.bfloat16)


def solution(mesh):
    in_specs = (
        P(("groups", "wide", "section"), "narrow"),
        P(("groups", "wide", "section"), None),
        P(("groups", "wide", "section"), None),
        P(("wide", "section"), None, "narrow"),
        P(("wide", "section"), None, "narrow"),
        P(("wide", "section"), None, "narrow"),
    )
    out_specs = P(("groups", "wide", "section"), "narrow")
    return jax.shard_map(shards, mesh=mesh, in_specs=in_specs, out_specs=out_specs, check_vma=False)
```

profile of v0, /device:TPU:0, one launch (start us, length us, event | category | flops | bytes accessed | tf_op | source)
XLA Modules:
  0.0 370.5 jit_solution(8743993185270205982)
XLA Ops:
  6.5 0.8 copy.38
  7.6 1.2 reduce-window.6
  8.8 0.2 slice_reduce_fusion
  9.0 0.1 fusion.18
  9.3 0.7 multiply_add_fusion
  10.1 0.5 fusion.14
  10.7 1.0 convolution_convert_fusion
  11.7 2.7 reshape.47
  14.4 4.0 %copy.44 = bf16[8,8,12,2048]{3,1,2,0:T(8,128)(2,1)S(1)} copy(bf16[8,8,12,2048]{3,2,1,0:T(8,128)(2,1)} %reshape.47) | data formatting | bytes 6291456 | tf_op jit(solution)/shard_map/reshape | solution.py:35
  18.4 77.7 %all_to_all.10 = bf16[8,8,12,2048]{3,1,2,0:T(8,128)(2,1)S(1)} all-to-all(bf16[8,8,12,2048]{3,1,2,0:T(8,128)(2,1)S(1)} %copy.44), channel_id=1, replica_groups=mesh['groups'=2,'wide'=4,'narrow'=2,'section'=2] {'wide','section'}, dimensions={0} | all-to-all | bytes 6291456 | tf_op jit(solution)/shard_map/all_to_all | solution.py:34
  96.0 3.8 %copy.45 = bf16[8,8,12,2048]{3,2,0,1:T(8,128)(2,1)} copy(bf16[8,8,12,2048]{3,1,2,0:T(8,128)(2,1)S(1)} %all_to_all.10) | data formatting | bytes 6291456 | tf_op jit(solution)/shard_map/all_to_all | solution.py:34
  99.8 0.2 all-gather.5.cloned.1.call-start
  100.1 102.8 %all-gather.3.cloned.1.call-done = bf16[8,8,12,4096]{3,2,0,1:T(8,128)(2,1)} async-done(((bf16[8,8,12,2048]{3,2,0,1:T(8,128)(2,1)}), bf16[8,8,12,4096]{3,2,0,1:T(8,128)(2,1)}) %all-gather.3.cloned.1.call-update) | async-done | bytes 6291472 | tf_op jit(solution)/shard_map/all_gather | solution.py:41
  202.9 15.2 %bitcast_multiply_fusion.1 = f32[8,8,12,384]{3,2,0,1:T(8,128)S(1)} fusion(bf16[8,8,12,4096]{3,2,0,1:T(8,128)(2,1)} %all-gather.3.cloned.1.call-done, bf16[8,4096,384]{2,1,0:T(8,128)(2,1)} %param.9), kind=kOutput, calls=%fused_computation.11 | convolution fusion | flops 2417098752 | bytes 32636928 | tf_op jit(solution)/shard_map/gjcd,jdf->gjcf/dot_general | solution.py:42
  218.1 16.1 %fusion.8 = bf16[8,8,12,384]{3,2,0,1:T(8,128)(2,1)} fusion(f32[8,8,12,384]{3,2,0,1:T(8,128)S(1)} %bitcast_multiply_fusion.1, bf16[8,8,12,4096]{3,2,0,1:T(8,128)(2,1)} %all-gather.3.cloned.1.call-done, bf16[8,4096,384]{2,1,0:T(8,128)(2,1)} %param.10), kind=kOutput, calls=%fused_computation.10 | convolution fusion | flops 2416508928 | bytes 33226752 | tf_op jit(solution)/shard_map/gjcd,jdf->gjcf/dot_general | solution.py:45
  234.2 27.3 %all-gather.5.cloned.1.call-done = bf16[8,8,12,768]{3,2,0,1:T(8,128)(2,1)} async-done(((bf16[8,8,12,384]{3,2,0,1:T(8,128)(2,1)}), bf16[8,8,12,768]{3,2,0,1:T(8,128)(2,1)}) %all-gather.5.cloned.1.call-update) | async-done | bytes 1179664 | tf_op jit(solution)/shard_map/all_gather | solution.py:49
  261.6 12.3 %convert_bitcast_fusion = bf16[8,8,12,2048]{3,2,0,1:T(8,128)(2,1)S(1)} fusion(bf16[8,8,12,768]{3,2,0,1:T(8,128)(2,1)} %all-gather.5.cloned.1.call-done, bf16[8,768,2048]{2,1,0:T(8,128)(2,1)} %param.11), kind=kOutput, calls=%fused_computation.6 | convolution fusion | flops 2417491968 | bytes 29491200 | tf_op jit(solution)/shard_map/gjcf,jfd->gjcd/dot_general | solution.py:47
  273.9 3.5 copy.46
  277.4 4.7 %all-to-all-start.1 = ((bf16[8,8,12,2048]{3,1,2,0:T(8,128)(2,1)}), bf16[8,8,12,2048]{3,1,2,0:T(8,128)(2,1)S(1)}, u32[]{:S(2)}, u32[]{:S(2)}) async-start(bf16[8,8,12,2048]{3,1,2,0:T(8,128)(2,1)} %copy.46), calls=%async_computation.1 | async-start | bytes 6291456 | tf_op jit(solution)/shard_map/all_to_all | solution.py:53
  282.2 0.6 select_reduce_fusion
  282.8 70.8 %all-to-all-done.1 = bf16[8,8,12,2048]{3,1,2,0:T(8,128)(2,1)S(1)} async-done(((bf16[8,8,12,2048]{3,1,2,0:T(8,128)(2,1)}), bf16[8,8,12,2048]{3,1,2,0:T(8,128)(2,1)S(1)}, u32[]{:S(2)}, u32[]{:S(2)}) %all-to-all-start.1) | async-done | bytes 3145760 | tf_op jit(solution)/shard_map/all_to_all | solution.py:53
  353.6 3.9 %copy.47 = bf16[8,8,12,2048]{3,2,1,0:T(8,128)(2,1)} copy(bf16[8,8,12,2048]{3,1,2,0:T(8,128)(2,1)S(1)} %all-to-all-done.1) | data formatting | bytes 6291456 | tf_op jit(solution)/shard_map/all_to_all | solution.py:53
  357.5 4.8 %reshape.48 = bf16[768,2048]{1,0:T(8,128)(2,1)S(1)} reshape(bf16[8,8,12,2048]{3,2,1,0:T(8,128)(2,1)} %copy.47) | data formatting | bytes 6291456 | tf_op jit(solution)/shard_map/reshape | solution.py:54
  362.2 1.4 convolution_convert_fusion.1
  (21 shorter events, 0.6 us)
Async XLA Ops:
  6.5 4.1 %copy-start = (bf16[64,2048]{1,0:T(8,128)(2,1)S(1)}, bf16[64,2048]{1,0:T(8,128)(2,1)}, u32[]{:S(2)}) copy-start(bf16[64,2048]{1,0:T(8,128)(2,1)} %param.6) | copy-start | bytes 786436
  6.5 196.4 %all-gather.3.cloned.1.call-start = ((), (), s32[]{:S(2)}) async-start(), calls=%async_computation.2 | async-start | bytes 12582912 | tf_op jit(solution)/shard_map/all_gather | solution.py:41
  99.8 161.7 %all-gather.5.cloned.1.call-start = ((), (), s32[]{:S(2)}) async-start(), calls=%async_computation.3 | async-start | bytes 2359296 | tf_op jit(solution)/shard_map/all_gather | solution.py:49
  277.4 4.7 %copy-start.2 = (f32[64,8]{0,1:T(8,128)S(1)}, f32[64,8]{0,1:T(8,128)}, u32[]{:S(2)}) copy-start(f32[64,8]{0,1:T(8,128)} %param.7) | copy-start | bytes 6148
  277.4 76.2 %all-to-all-start.1 = ((bf16[8,8,12,2048]{3,1,2,0:T(8,128)(2,1)}), bf16[8,8,12,2048]{3,1,2,0:T(8,128)(2,1)S(1)}, u32[]{:S(2)}, u32[]{:S(2)}) async-start(bf16[8,8,12,2048]{3,1,2,0:T(8,128)(2,1)} %copy.46), calls=%async_computation.1 | async-start | bytes 6291456 | tf_op jit(solution)/shard_map/all_to_all | solution.py:53
  357.5 6.1 %copy-start.1 = (bf16[64,2048]{1,0:T(8,128)(2,1)S(1)}, bf16[64,2048]{1,0:T(8,128)(2,1)}, u32[]{:S(2)}) copy-start(bf16[64,2048]{1,0:T(8,128)(2,1)} %param.6) | copy-start | bytes 786436
Sparse Core Ops, SparseCore 0:
  99.9 102.9 all-gather.2
  234.3 27.1 all-gather.4
where the time goes:
time: 371 us; the launch traced here: 370 us
  waiting for transfers between devices  201 us (54%)
  blocking collectives  77.7 us (21%)
  matrix products  46 us (12%)
  local copies, waits for them, and re-layouts  24.1 us (6%)
  between operations  13.5 us (4%)
  starting transfers between devices  4.97 us (1%)
    all_gather x1, waiting for transfers between devices, shards(): portion = lax.all_gather(arrived, 'narrow', axis=3, tiled=True)  103 us
    all_to_all x1, blocking collectives, shards(): lax.all_to_all(outgoing.reshape(owners, per_owner, CAP, feature_part), ('...  77.7 us
    all_to_all x1, waiting for transfers between devices, shards(): lax.all_to_all(summed, ('wide', 'section'), split_axis=0, concat_axis=0,...  70.8 us
    all_gather x1, waiting for transfers between devices, shards(): lax.all_gather(hidden, 'narrow', axis=3, tiled=True)  27.3 us
    dot_general x1, matrix products, shards(): jnp.einsum('gjcd,jdf->gjcf', portion, up_weight, preferred_element_type=j...  16.1 us
    dot_general x1, matrix products, shards(): jnp.einsum('gjcd,jdf->gjcf', portion, gate_weight, preferred_element_type...  15.2 us
    dot_general x1, matrix products, shards(): jnp.einsum('gjcf,jfd->gjcd', lax.all_gather(hidden, 'narrow', axis=3, til...  12.3 us
  transfers between devices with their start and end apart: 3, of which 3 were waited for; matrix products, arithmetic and copies ran while one was open for 0% of the time, Pallas kernels for 0%

commit v1 on v0

--- a/solution.py
+++ b/solution.py
@@ -4,6 +4,31 @@
 from jax.sharding import PartitionSpec as P
 
 CAP = 12
+
+
+def get_tokens_now(shard_in):
+    axis_name = "narrow"
+    known, vec_out, last = (
+        jax.lax.axis_size(axis_name),
+        jax.lax.axis_index(axis_name),
+        shard_in.shape[3],
+    )
+    right_arr, q_next = (shard_in, 1)
+    while q_next < known:
+        right_arr = jnp.concatenate(
+            [
+                right_arr,
+                jax.lax.ppermute(
+                    right_arr,
+                    axis_name=axis_name,
+                    perm=[(j0, (j0 - q_next) % known) for j0 in range(known)],
+                ),
+            ],
+            axis=3,
+        )
+        q_next = 2 * q_next
+    clean = jnp.roll(right_arr, vec_out * last, axis=3)
+    return clean
 
 
 def shards(tokens, route_logits, expert_ids, gate_weight, up_weight, down_weight):
@@ -45,10 +70,7 @@
     up_add = jnp.einsum("gjcd,jdf->gjcf", portion, up_weight, preferred_element_type=jnp.float32)
     hidden = (jax.nn.silu(gate_add) * up_add).astype(jnp.bfloat16)
     summed = jnp.einsum(
-        "gjcf,jfd->gjcd",
-        lax.all_gather(hidden, "narrow", axis=3, tiled=True),
-        down_weight,
-        preferred_element_type=jnp.float32,
+        "gjcf,jfd->gjcd", get_tokens_now(hidden), down_weight, preferred_element_type=jnp.float32
     ).astype(jnp.bfloat16)
     returned = lax.all_to_all(summed, ("wide", "section"), split_axis=0, concat_axis=0, tiled=True)
     returned = returned.reshape(experts * CAP, feature_part)

time: 371 us -> 364 us (0.981)
  waiting for transfers between devices: 201 us -> 188 us
    all_gather x1 -> x0, waiting for transfers between devices: 27.3 us -> none  [shards(): lax.all_gather(hidden, 'narrow', axis=3, tiled=True)]
    ppermute x0 -> x1, waiting for transfers between devices: none -> 14.6 us  [get_tokens_now(): jax.lax.ppermute(right_arr, axis_name=axis_name, perm=[(j0, (j0 - q_next)...]
where the time goes in v1:
time: 364 us; the launch traced here: 363 us
  waiting for transfers between devices  188 us (52%)
  blocking collectives  77.7 us (21%)
  matrix products  48.3 us (13%)
  local copies, waits for them, and re-layouts  26.9 us (7%)
  between operations  13.5 us (4%)
  starting transfers between devices  5.15 us (1%)
    all_gather x1, waiting for transfers between devices, shards(): portion = lax.all_gather(arrived, 'narrow', axis=3, tiled=True)  103 us
    all_to_all x1, blocking collectives, shards(): lax.all_to_all(outgoing.reshape(owners, per_owner, CAP, feature_part), ('...  77.7 us
    all_to_all x1, waiting for transfers between devices, shards(): lax.all_to_all(summed, ('wide', 'section'), split_axis=0, concat_axis=0,...  70.8 us
    dot_general x1, matrix products, shards(): jnp.einsum('gjcf,jfd->gjcd', get_tokens_now(hidden), down_weight, preferr...  15.6 us
    dot_general x1, matrix products, shards(): jnp.einsum('gjcd,jdf->gjcf', portion, gate_weight, preferred_element_type...  15.2 us
    dot_general x1, matrix products, shards(): jnp.einsum('gjcd,jdf->gjcf', portion, up_weight, preferred_element_type=j...  15.1 us
    ppermute x1, waiting for transfers between devices, get_tokens_now(): jax.lax.ppermute(right_arr, axis_name=axis_name, perm=[(j0, (j0 - q_next)...  14.6 us
  transfers between devices with their start and end apart: 3, of which 3 were waited for; matrix products, arithmetic and copies ran while one was open for 0% of the time, Pallas kernels for 0%

profile of v1, /device:TPU:0, one launch (start us, length us, event | category | flops | bytes accessed | tf_op | source)
XLA Modules:
  0.0 363.2 jit_solution(5777854912567323225)
XLA Ops:
  6.5 0.8 copy.44
  7.6 1.2 reduce-window.6
  8.8 0.2 slice_reduce_fusion
  9.3 0.7 multiply_add_fusion
  10.1 0.5 fusion.18
  10.7 1.0 convolution_convert_fusion
  11.7 2.7 reshape.47
  14.4 4.0 %copy.50 = bf16[8,8,12,2048]{3,1,2,0:T(8,128)(2,1)S(1)} copy(bf16[8,8,12,2048]{3,2,1,0:T(8,128)(2,1)} %reshape.47) | data formatting | bytes 6291456 | tf_op jit(solution)/shard_map/reshape | solution.py:60
  18.4 77.7 %all_to_all.10 = bf16[8,8,12,2048]{3,1,2,0:T(8,128)(2,1)S(1)} all-to-all(bf16[8,8,12,2048]{3,1,2,0:T(8,128)(2,1)S(1)} %copy.50), channel_id=1, replica_groups=mesh['groups'=2,'wide'=4,'narrow'=2,'section'=2] {'wide','section'}, dimensions={0} | all-to-all | bytes 6291456 | tf_op jit(solution)/shard_map/all_to_all | solution.py:59
  96.0 3.8 %copy.51 = bf16[8,8,12,2048]{3,2,0,1:T(8,128)(2,1)} copy(bf16[8,8,12,2048]{3,1,2,0:T(8,128)(2,1)S(1)} %all_to_all.10) | data formatting | bytes 6291456 | tf_op jit(solution)/shard_map/all_to_all | solution.py:59
  99.8 103.1 %all-gather.2.cloned.1.call-done = bf16[8,8,12,4096]{3,2,0,1:T(8,128)(2,1)} async-done(((bf16[8,8,12,2048]{3,2,0,1:T(8,128)(2,1)}), bf16[8,8,12,4096]{3,2,0,1:T(8,128)(2,1)}) %all-gather.2.cloned.1.call-update) | async-done | bytes 6291472 | tf_op jit(solution)/shard_map/all_gather | solution.py:66
  202.9 15.2 %bitcast_multiply_fusion.1 = f32[8,8,12,384]{3,2,0,1:T(8,128)S(1)} fusion(bf16[8,8,12,4096]{3,2,0,1:T(8,128)(2,1)} %all-gather.2.cloned.1.call-done, bf16[8,4096,384]{2,1,0:T(8,128)(2,1)} %param.9), kind=kOutput, calls=%fused_computation.18 | convolution fusion | flops 2417098752 | bytes 32636928 | tf_op jit(solution)/shard_map/gjcd,jdf->gjcf/dot_general | solution.py:67
  218.1 15.1 %fusion.12 = bf16[8,8,12,384]{3,2,0,1:T(8,128)(2,1)S(1)} fusion(f32[8,8,12,384]{3,2,0,1:T(8,128)S(1)} %bitcast_multiply_fusion.1, bf16[8,8,12,4096]{3,2,0,1:T(8,128)(2,1)} %all-gather.2.cloned.1.call-done, bf16[8,4096,384]{2,1,0:T(8,128)(2,1)} %param.10), kind=kOutput, calls=%fused_computation.17 | convolution fusion | flops 2416508928 | bytes 33226752 | tf_op jit(solution)/shard_map/gjcd,jdf->gjcf/dot_general | solution.py:70
  233.3 0.3 copy.52
  233.6 0.4 collective-permute-start
  234.0 14.6 %collective-permute-done = bf16[8,8,12,384]{3,1,2,0:T(8,128)(2,1)S(1)} collective-permute-done((bf16[8,8,12,384]{3,1,2,0:T(8,128)(2,1)S(1)}, bf16[8,8,12,384]{3,1,2,0:T(8,128)(2,1)S(1)}, u32[]{:S(2)}, u32[]{:S(2)}) %collective-permute-start) | collective-permute-done | bytes 589856 | tf_op jit(solution)/shard_map/ppermute | solution.py:21
  248.7 15.6 %convert_bitcast_fusion = bf16[8,8,12,2048]{3,2,0,1:T(8,128)(2,1)} fusion(bf16[8,768,2048]{2,1,0:T(8,128)(2,1)} %param.11, s32[]{:T(128)S(6)} %select_n.19, bf16[8,8,12,384]{3,2,0,1:T(8,128)(2,1)S(1)} %fusion.12, bf16[8,8,12,384]{3,2,0,1:T(8,128)(2,1)S(1)} %copy.53), kind=kOutput, calls=%fused_computation.6 | convolution fusion | flops 2422210560 | bytes 29491204 | tf_op jit(solution)/shard_map/gjcf,jfd->gjcd/dot_general | solution.py:72
  264.3 5.9 %copy.55 = bf16[8,8,12,2048]{3,1,2,0:T(8,128)(2,1)} copy(bf16[8,8,12,2048]{3,2,0,1:T(8,128)(2,1)} %convert_bitcast_fusion) | data formatting | bytes 6291456 | tf_op jit(solution)/shard_map/convert_element_type | solution.py:74
  270.1 4.7 %all-to-all-start.1 = ((bf16[8,8,12,2048]{3,1,2,0:T(8,128)(2,1)}), bf16[8,8,12,2048]{3,1,2,0:T(8,128)(2,1)S(1)}, u32[]{:S(2)}, u32[]{:S(2)}) async-start(bf16[8,8,12,2048]{3,1,2,0:T(8,128)(2,1)} %copy.55), calls=%async_computation.1 | async-start | bytes 6291456 | tf_op jit(solution)/shard_map/all_to_all | solution.py:75
  275.0 0.6 select_reduce_fusion
  275.6 70.8 %all-to-all-done.1 = bf16[8,8,12,2048]{3,1,2,0:T(8,128)(2,1)S(1)} async-done(((bf16[8,8,12,2048]{3,1,2,0:T(8,128)(2,1)}), bf16[8,8,12,2048]{3,1,2,0:T(8,128)(2,1)S(1)}, u32[]{:S(2)}, u32[]{:S(2)}) %all-to-all-start.1) | async-done | bytes 3145760 | tf_op jit(solution)/shard_map/all_to_all | solution.py:75
  346.4 3.9 %copy.56 = bf16[8,8,12,2048]{3,2,1,0:T(8,128)(2,1)} copy(bf16[8,8,12,2048]{3,1,2,0:T(8,128)(2,1)S(1)} %all-to-all-done.1) | data formatting | bytes 6291456 | tf_op jit(solution)/shard_map/all_to_all | solution.py:75
  350.2 4.8 %reshape.48 = bf16[768,2048]{1,0:T(8,128)(2,1)S(1)} reshape(bf16[8,8,12,2048]{3,2,1,0:T(8,128)(2,1)} %copy.56) | data formatting | bytes 6291456 | tf_op jit(solution)/shard_map/reshape | solution.py:76
  355.0 1.4 convolution_convert_fusion.1
  (22 shorter events, 0.9 us)
Async XLA Ops:
  6.5 4.1 %copy-start = (bf16[64,2048]{1,0:T(8,128)(2,1)S(1)}, bf16[64,2048]{1,0:T(8,128)(2,1)}, u32[]{:S(2)}) copy-start(bf16[64,2048]{1,0:T(8,128)(2,1)} %param.6) | copy-start | bytes 786436
  6.5 196.4 %all-gather.2.cloned.1.call-start = ((), (), s32[]{:S(2)}) async-start(), calls=%async_computation.2 | async-start | bytes 12582912 | tf_op jit(solution)/shard_map/all_gather | solution.py:66
  233.6 15.0 %collective-permute-start = (bf16[8,8,12,384]{3,1,2,0:T(8,128)(2,1)S(1)}, bf16[8,8,12,384]{3,1,2,0:T(8,128)(2,1)S(1)}, u32[]{:S(2)}, u32[]{:S(2)}) collective-permute-start(bf16[8,8,12,384]{3,1,2,0:T(8,128)(2,1)S(1)} %copy.52), channel_id=1, source_target_pairs={{0,2},{2,0},{1,3},{3,1},{4,6},{6,4},{5,7},{7,5},{8,10},{10,8},{9,1... | collective-permute-start | bytes 1769480 | tf_op jit(solution)/shard_map/ppermute | solution.py:21
  270.1 4.7 %copy-start.2 = (f32[64,8]{0,1:T(8,128)S(1)}, f32[64,8]{0,1:T(8,128)}, u32[]{:S(2)}) copy-start(f32[64,8]{0,1:T(8,128)} %param.7) | copy-start | bytes 6148
  270.1 76.2 %all-to-all-start.1 = ((bf16[8,8,12,2048]{3,1,2,0:T(8,128)(2,1)}), bf16[8,8,12,2048]{3,1,2,0:T(8,128)(2,1)S(1)}, u32[]{:S(2)}, u32[]{:S(2)}) async-start(bf16[8,8,12,2048]{3,1,2,0:T(8,128)(2,1)} %copy.55), calls=%async_computation.1 | async-start | bytes 6291456 | tf_op jit(solution)/shard_map/all_to_all | solution.py:75
  350.2 6.1 %copy-start.1 = (bf16[64,2048]{1,0:T(8,128)(2,1)S(1)}, bf16[64,2048]{1,0:T(8,128)(2,1)}, u32[]{:S(2)}) copy-start(bf16[64,2048]{1,0:T(8,128)(2,1)} %param.6) | copy-start | bytes 786436
Sparse Core Ops, SparseCore 0:
  99.9 102.9 all-gather.1
